TPU v7x, 32 devices: a whole 2x2x4 slice. The times are simulated.
32 devices in a mesh: region: 4 (over z), row: 2 (over core), col: 4 (over y, x).
Axes of the slice: x: 2, y: 2, z: 4, core: 2. Of those that a mesh axis runs over, the one named last changes fastest.
Arguments:
- cam_jac: bfloat16 [3, 2, 256, 16384], P(None, None, None, 'region'), may hold values from -1 to 1
- point_rows: bfloat16 [3, 2, 4, 16384], P(None, None, None, 'region'), may hold values from -6 to 6
- track_images: int32 [3, 16384], P(None, 'region'), may hold values from 0 to 3, as said below
- track_counts: int32 [4], replicated, may hold values from 1 to 4096, 8192 in all
Outputs:
- factor: float32 [1024, 1024], P(('region', 'row'), 'col')
- solved: float32 [1024], replicated
Inputs may be any that keep to these rules, and one draw needn't show every extreme that they name: `track_images`: each track's 3 entries are different images of the slab. `track_counts`: entry r counts region r's live tracks, which fill its first slots; later slots hold data that no output reads. The counts sum to 8192, and one region has exactly 4096.
All inputs are finite; a program needn't handle non-finite values.
Results may differ from a plain program's by a relative error of at most 0.0036.
Values may be sent and summed in bfloat16 or wider, within the bound.
A program may use at most 128 MiB of HBM per device.

v0:
```python
import jax
import jax.numpy as jnp
from jax import lax
from jax.sharding import PartitionSpec as P

SLAB_IMAGES = 4
BLOCK = 256
damping = 0.1
point_damping = 0.5


def from_root(value, axis, source):
    kept = jnp.where(lax.axis_index(axis) == source, value, 0).astype(value.dtype)
    return lax.psum(kept, axis)


def lower_solve(factor_parts, first, second, third):
    diag_one, below_one, diag_two, below_far, below_two, diag_three = factor_parts
    out_one = first / diag_one
    out_two = (second - below_one * out_one) / diag_two
    out_three = (third - below_far * out_one - below_two * out_two) / diag_three
    return (out_one, out_two, out_three)


def block_terms(cam, points, selector):
    jac_point = points[:, :, 0:3].astype(jnp.float32)
    errors = points[:, :, 3].astype(jnp.float32)

    def entry(left, right):
        return jnp.sum(jac_point[:, :, left] * jac_point[:, :, right], axis=(0, 1))

    diag_one = jnp.sqrt(entry(0, 0) + point_damping)
    below_one = entry(1, 0) / diag_one
    below_far = entry(2, 0) / diag_one
    diag_two = jnp.sqrt(entry(1, 1) + point_damping - below_one * below_one)
    below_two = (entry(2, 1) - below_far * below_one) / diag_two
    diag_three = jnp.sqrt(
        entry(2, 2) + point_damping - below_far * below_far - below_two * below_two
    )
    factor_parts = (diag_one, below_one, diag_two, below_far, below_two, diag_three)
    coef = jnp.stack(
        lower_solve(factor_parts, jac_point[:, :, 0], jac_point[:, :, 1], jac_point[:, :, 2]),
        axis=0,
    ).astype(jnp.bfloat16)
    grads = [jnp.sum(jac_point[:, :, comp] * errors, axis=(0, 1)) for comp in range(3)]
    point_step = jnp.stack(lower_solve(factor_parts, grads[0], grads[1], grads[2]), axis=0).astype(
        jnp.bfloat16
    )
    coef_wide = coef.astype(jnp.float32)
    products = (
        cam[:, 0, :, None, :].astype(jnp.float32)
        * coef_wide[:, :, 0, :].transpose(1, 0, 2)[:, None, :, :]
    )
    products = (
        products
        + cam[:, 1, :, None, :].astype(jnp.float32)
        * coef_wide[:, :, 1, :].transpose(1, 0, 2)[:, None, :, :]
    )
    schur = selector[0][:, None, None, :] * products[0][None]
    for view in range(1, selector.shape[0]):
        schur = schur + selector[view][:, None, None, :] * products[view][None]
    schur = schur.astype(jnp.bfloat16)
    pick = selector.astype(jnp.bfloat16)
    diagonal = jnp.einsum("krpb,kab->aprb", cam, pick, preferred_element_type=jnp.float32).astype(
        jnp.bfloat16
    )
    err_pick = (errors[None, :, :, :] * selector.transpose(1, 0, 2)[:, :, None, :]).astype(
        jnp.bfloat16
    )
    direct = jnp.einsum("krpb,akrb->ap", cam, err_pick, preferred_element_type=jnp.float32)
    coupled = jnp.einsum("apmb,mb->ap", schur, point_step, preferred_element_type=jnp.float32)
    return (schur, diagonal, direct - coupled)


def panel_factor(column, first_row, end_row):
    chol_block = jnp.linalg.cholesky(column[first_row:end_row])
    parts = [jnp.zeros((first_row, column.shape[1]), column.dtype), chol_block]
    if end_row < column.shape[0]:
        parts.append(
            lax.linalg.triangular_solve(
                chol_block, column[end_row:], left_side=False, lower=True, transpose_a=True
            )
        )
    return jnp.concatenate(parts, axis=0)


def on_device(cam_jac, point_rows, track_images, track_counts):
    regions = lax.axis_size("region")
    row_count = lax.axis_size("row")
    region_at = lax.axis_index("region")
    row_at = lax.axis_index("row")
    col_at = lax.axis_index("col")
    params = cam_jac.shape[2]
    slots = cam_jac.shape[3]
    total_cols = SLAB_IMAGES * params
    row_block = total_cols // (regions * row_count)
    images = track_images.astype(jnp.float32)
    live = (jnp.arange(slots, dtype=jnp.int32) < track_counts[region_at]).astype(jnp.float32)
    depth = live.shape[0]
    tile_rows = regions * row_block
    share = params // row_count
    contract = (((1,), (1,)), ((), ()))

    def block_step(block, carry):
        tile_acc, grad_acc = carry
        start = block * BLOCK
        cam = lax.dynamic_slice_in_dim(cam_jac, start, BLOCK, 3)
        pts = lax.dynamic_slice_in_dim(point_rows, start, BLOCK, 3)
        block_images = lax.dynamic_slice_in_dim(images, start, BLOCK, 1)
        alive = lax.dynamic_slice_in_dim(live, start, BLOCK, 0)
        selector = (
            block_images[:, None, :] == jnp.arange(SLAB_IMAGES, dtype=jnp.float32)[None, :, None]
        ).astype(jnp.float32) * alive[None, None, :]
        schur, diagonal, grad = block_terms(cam, pts, selector)
        schur_grid = schur.reshape(regions, row_count, row_block, 3 * BLOCK)
        row_part = lax.dynamic_index_in_dim(schur_grid, row_at, 1, keepdims=False).reshape(
            tile_rows, 3 * BLOCK
        )
        col_part = lax.dynamic_index_in_dim(schur, col_at, 0, keepdims=False).reshape(
            params, 3 * BLOCK
        )
        tile_acc = tile_acc - lax.dot_general(
            row_part, col_part, contract, preferred_element_type=jnp.float32
        )
        diag_grid = diagonal.reshape(regions, row_count, row_block, 2 * BLOCK)
        diag_rows = lax.dynamic_index_in_dim(diag_grid, row_at, 1, keepdims=False).reshape(
            tile_rows, 2 * BLOCK
        )
        diag_rows = lax.dynamic_slice_in_dim(diag_rows, col_at * share, share, 0)
        diag_col = lax.dynamic_index_in_dim(diagonal, col_at, 0, keepdims=False).reshape(
            params, 2 * BLOCK
        )
        update = lax.dot_general(diag_rows, diag_col, contract, preferred_element_type=jnp.float32)
        current = lax.dynamic_slice_in_dim(tile_acc, col_at * share, share, 0)
        tile_acc = lax.dynamic_update_slice_in_dim(tile_acc, current + update, col_at * share, 0)
        grad_acc = grad_acc + lax.dynamic_index_in_dim(grad, col_at, 0, keepdims=False)
        return (tile_acc, grad_acc)

    start_state = (jnp.zeros((tile_rows, params), jnp.float32), jnp.zeros((params,), jnp.float32))
    tile_acc, grad_acc = lax.fori_loop(0, depth // BLOCK, block_step, start_state)
    held, grad_piece = (
        lax.psum_scatter(tile_acc, "region", scatter_dimension=0, tiled=True),
        lax.psum_scatter(
            grad_acc.reshape(regions, params // regions), "region", scatter_dimension=0, tiled=True
        ),
    )
    gathered = lax.all_gather(grad_piece, ("region", "col"), axis=0, tiled=True)
    gradient = (
        gathered.reshape(regions, SLAB_IMAGES, params // regions)
        .transpose(1, 0, 2)
        .reshape(total_cols)
    )
    row_start = (region_at * row_count + row_at) * row_block
    global_rows = row_start + jnp.arange(row_block, dtype=jnp.int32)
    global_cols = col_at * params + jnp.arange(params, dtype=jnp.int32)
    held = held + damping * (global_rows[:, None] == global_cols[None, :]).astype(jnp.float32)
    factor_mine = jnp.zeros((row_block, params), jnp.float32)
    pieces = []
    for panel in range(SLAB_IMAGES):
        first_row = panel * params
        end_row = first_row + params
        column = lax.all_gather(held, ("region", "row"), axis=0, tiled=True)
        factored = lax.cond(
            col_at == panel,
            lambda whole: panel_factor(whole, first_row, end_row),
            lambda whole: jnp.zeros_like(whole),
            column,
        )
        factored = from_root(factored, "col", panel)
        mine = lax.dynamic_slice_in_dim(factored, row_start, row_block, 0)
        partner = lax.dynamic_slice_in_dim(factored, col_at * params, params, 0)
        held = held - jnp.dot(mine, partner.T, precision=lax.Precision.HIGHEST)
        factor_mine = jnp.where(col_at == panel, mine, factor_mine)
        part_z = lax.linalg.triangular_solve(
            factored[first_row:end_row],
            gradient[first_row:end_row][:, None],
            left_side=True,
            lower=True,
        )[:, 0]
        pieces.append(part_z)
        below = jnp.concatenate(
            [jnp.zeros((end_row, params), jnp.float32), factored[end_row:]], axis=0
        )
        gradient = gradient - jnp.dot(below, part_z, precision=lax.Precision.HIGHEST)
    return (factor_mine, jnp.concatenate(pieces))


def solution(mesh):
    in_specs = (
        P(None, None, None, "region"),
        P(None, None, None, "region"),
        P(None, "region"),
        P(),
    )
    out_specs = (P(("region", "row"), "col"), P())
    return jax.shard_map(
        on_device, mesh=mesh, in_specs=in_specs, out_specs=out_specs, check_vma=False
    )
```

profile of v0, /device:TPU:0, one launch (start us, length us, event | category | flops | bytes accessed | tf_op | source)
XLA Modules:
  0.0 1097.6 jit_solution(16919428303074503304)
XLA Ops:
  11.4 459.7 %while.32 = (s32[]{:T(128)}, f32[512,256]{1,0:T(8,128)}, f32[256]{0:T(256)}, f32[3,4096]{1,0:T(4,128)S(1)}, f32[4096]{0:T(1024)}, /*index=5*/bf16[3,2,256,4096]{...) while((s32[]{:T(128)}, f32[512,256]{1,0:T(8,128)}, ...), condition=%wide.region_10.11_spmd.clone, body=%wide.region_0.10_spmd.clone.sunk | while | flops 252784384 | bytes 64036492 | solution.py:140
  308.5 1.9 copy.167
  452.2 1.9 copy.167
  471.3 24.6 %reduce-scatter.2.cloned.1.call-done = f32[128,256]{1,0:T(8,128)} async-done(((f32[512,256]{1,0:T(8,128)}), f32[128,256]{1,0:T(8,128)}) %reduce-scatter.2.cloned.1.call-update) | async-done | bytes 131088 | tf_op jit(solution)/shard_map/reduce_scatter | solution.py:142
  497.6 21.0 %all-gather.6.cloned.1.call-done = f32[1024,256]{1,0:T(8,128)} async-done(((f32[128,256]{1,0:T(8,128)}), f32[1024,256]{1,0:T(8,128)}) %all-gather.6.cloned.1.call-update) | async-done | bytes 1048592 | tf_op jit(solution)/shard_map/all_gather | solution.py:162
  518.6 64.9 %conditional.4 = (f32[1024,256]{1,0:T(8,128)S(1)}) conditional(s32[]{:T(128)} %convert_element_type.162, () %tuple.57, f32[1024,256]{1,0:T(8,128)} %all-gather.6.cloned.1.call-done), branch_computations={%region_12.13_spmd, %region_13.0_spmd} | conditional | flops 504480000 | bytes 15862003 | solution.py:163
  521.4 11.7 %cholesky.214 = f32[128,128]{1,0:T(8,128)S(1)} custom-call(f32[128,128]{1,0:T(8,128)S(1)} %cholesky.346), custom_call_target="Cholesky" | custom-call | tf_op jit(solution)/shard_map/cond/branch_1_fun/jit(cholesky)/cholesky | solution.py:76
  533.1 9.8 custom-call.27
  543.4 11.7 %cholesky.231 = f32[128,128]{1,0:T(8,128)S(1)} custom-call(f32[128,128]{1,0:T(8,128)S(1)} %convolution_subtract_fusion.1), custom_call_target="Cholesky" | custom-call | tf_op jit(solution)/shard_map/cond/branch_1_fun/jit(cholesky)/cholesky | solution.py:76
  557.3 4.0 while.29
  561.3 19.7 %custom-call.16 = f32[2,128,128]{1,2,0:T(8,128)S(1)} custom-call(f32[2,128,128]{2,1,0:T(8,128)S(1)} %get-tuple-element.256), custom_call_target="InvertDiagBlocksLowerTriangular" | custom-call | tf_op jit(solution)/shard_map/cond/branch_1_fun/triangular_solve | solution.py:80
  584.7 50.4 %all-reduce.11.cloned.1.call-done = f32[1024,256]{1,0:T(8,128)} async-done(((f32[1024,256]{1,0:T(8,128)}), f32[1024,256]{1,0:T(8,128)}) %all-reduce.11.cloned.1.call-update) | async-done | bytes 1048592 | tf_op jit(solution)/shard_map/psum | solution.py:14
  635.1 2.1 convolution_subtract_fusion.10
  637.2 22.3 %all-gather.8.cloned.1.call-done = f32[1024,256]{1,0:T(8,128)} async-done(((f32[128,256]{1,0:T(8,128)}), f32[1024,256]{1,0:T(8,128)}) %all-gather.8.cloned.1.call-update) | async-done | bytes 1048592 | tf_op jit(solution)/shard_map/all_gather | solution.py:162
  659.6 8.2 conditional.5
  669.0 107.6 %all-reduce.13.cloned.1.call-done = f32[1024,256]{1,0:T(8,128)} async-done(((f32[1024,256]{1,0:T(8,128)}), f32[1024,256]{1,0:T(8,128)}) %all-reduce.13.cloned.1.call-update) | async-done | bytes 1048592 | tf_op jit(solution)/shard_map/psum | solution.py:14
  776.6 2.1 convolution_subtract_fusion.9
  779.4 11.7 %all-reduce.5 = f32[4,64]{1,0:T(4,128)S(1)} all-reduce(f32[4,64]{1,0:T(4,128)S(1)} %reshape.640), channel_id=3, replica_groups=mesh['region'=4,'row'=2,'col'=4] {'region'}, use_global_device_ids=true, to_apply=%region_28.30.clone | all-reduce | flops 256 | bytes 2048
  791.7 37.0 %all-gather = f32[16,1,64]{2,1,0:T(1,128)S(1)} all-gather(f32[1,1,64]{2,1,0:T(1,128)S(1)} %dynamic-slice_bitcast_fusion.1), channel_id=1, replica_groups=mesh['region'=4,'row'=2,'col'=4] {'region','col'}, dimensions={0}, use_global_device_ids=true | all-gather | bytes 4352 | tf_op jit(solution)/shard_map/all_gather | solution.py:147
  828.9 5.6 conditional.6
  835.7 3.9 while.33
  839.6 19.7 %custom-call.31 = f32[2,128,128]{1,2,0:T(8,128)S(1)} custom-call(f32[2,128,128]{2,1,0:T(8,128)S(1)} %get-tuple-element.332), custom_call_target="InvertDiagBlocksLowerTriangular" | custom-call | tf_op jit(solution)/shard_map/triangular_solve/custom-call.6 | solution.py:174
  860.7 82.2 %all-reduce.15.cloned.1.call-done = f32[1024,256]{1,0:T(8,128)} async-done(((f32[1024,256]{1,0:T(8,128)}), f32[1024,256]{1,0:T(8,128)}) %all-reduce.15.cloned.1.call-update) | async-done | bytes 1048592 | tf_op jit(solution)/shard_map/psum | solution.py:14
  942.9 2.1 convolution_subtract_fusion.8
  945.1 3.8 while.34
  948.9 19.7 %custom-call.32 = f32[2,128,128]{1,2,0:T(8,128)S(1)} custom-call(f32[2,128,128]{2,1,0:T(8,128)S(1)} %get-tuple-element.333), custom_call_target="InvertDiagBlocksLowerTriangular" | custom-call | tf_op jit(solution)/shard_map/triangular_solve/custom-call.6 | solution.py:174
  970.9 4.8 conditional.7
  976.8 4.0 while.35
  980.8 19.7 %custom-call.33 = f32[2,128,128]{1,2,0:T(8,128)S(1)} custom-call(f32[2,128,128]{2,1,0:T(8,128)S(1)} %get-tuple-element.334), custom_call_target="InvertDiagBlocksLowerTriangular" | custom-call | tf_op jit(solution)/shard_map/triangular_solve/custom-call.6 | solution.py:174
  1001.4 61.7 %all-reduce.17.cloned.1.call-done = f32[1024,256]{1,0:T(8,128)} async-done(((f32[1024,256]{1,0:T(8,128)}), f32[1024,256]{1,0:T(8,128)}) %all-reduce.17.cloned.1.call-update) | async-done | bytes 1048592 | tf_op jit(solution)/shard_map/psum | solution.py:14
  1064.2 4.0 while.36
  1068.2 19.7 %custom-call.34 = f32[2,128,128]{1,2,0:T(8,128)S(1)} custom-call(f32[2,128,128]{2,1,0:T(8,128)S(1)} %get-tuple-element.335), custom_call_target="InvertDiagBlocksLowerTriangular" | custom-call | tf_op jit(solution)/shard_map/triangular_solve/custom-call.6 | solution.py:174
  (1506 shorter events, 495.8 us)
Async XLA Ops:
  7.2 488.7 %reduce-scatter.2.cloned.1.call-start = ((), (), s32[]{:S(2)}) async-start(), calls=%async_computation.1 | async-start | bytes 655360 | tf_op jit(solution)/shard_map/reduce_scatter | solution.py:142
  11.4 5.8 copy-start.17
  40.1 5.8 copy-start.17
  68.9 5.8 copy-start.17
  97.7 5.8 copy-start.17
  126.4 5.8 copy-start.17
  155.1 5.8 copy-start.17
  183.9 5.8 copy-start.17
  212.6 5.8 copy-start.17
  270.1 5.8 copy-start.17
  327.5 5.8 copy-start.17
  356.2 5.8 copy-start.17
  385.0 5.8 copy-start.17
  413.7 5.8 copy-start.17
  442.4 5.8 copy-start.17
  471.2 47.4 %all-gather.6.cloned.1.call-start = ((), (), s32[]{:S(2)}) async-start(), calls=%async_computation.2 | async-start | bytes 1179648 | tf_op jit(solution)/shard_map/all_gather | solution.py:162
  497.6 137.5 %all-reduce.11.cloned.1.call-start = ((), (), s32[]{:S(2)}) async-start(), calls=%async_computation.3 | async-start | bytes 2097152 | tf_op jit(solution)/shard_map/psum | solution.py:14
  520.1 60.9 %copy-start.7 = (f32[1024,256]{1,0:T(8,128)S(1)}, f32[1024,256]{1,0:T(8,128)}, u32[]{:S(2)}) copy-start(f32[1024,256]{1,0:T(8,128)} %param.4) | copy-start | bytes 3145732 | tf_op jit(solution)/shard_map/cond
  583.5 51.6 %copy-start.10 = (f32[128,256]{1,0:T(8,128)S(1)}, f32[128,256]{1,0:T(8,128)}, u32[]{:S(2)}) copy-start(f32[128,256]{1,0:T(8,128)} %select_add_fusion.1) | copy-start | bytes 393220
  584.6 75.0 %all-gather.8.cloned.1.call-start = ((), (), s32[]{:S(2)}) async-start(), calls=%async_computation.4 | async-start | bytes 1179648 | tf_op jit(solution)/shard_map/all_gather | solution.py:162
  637.2 139.4 %all-reduce.13.cloned.1.call-start = ((), (), s32[]{:S(2)}) async-start(), calls=%async_computation.5 | async-start | bytes 2097152 | tf_op jit(solution)/shard_map/psum | solution.py:14
  667.8 108.8 %copy-start.9 = (f32[128,256]{1,0:T(8,128)S(1)}, f32[128,256]{1,0:T(8,128)}, u32[]{:S(2)}) copy-start(f32[128,256]{1,0:T(8,128)} %convolution_subtract_fusion.10) | copy-start | bytes 393220
  667.8 110.9 %copy-start.21 = (f32[256]{0:T(256)S(1)}, f32[256]{0:T(256)}, u32[]{:S(2)}) copy-start(f32[256]{0:T(256)} %get-tuple-element.248) | copy-start | bytes 3076
  667.8 111.0 %copy-start.22 = (u32[32]{0:T(128)S(1)}, u32[32]{0:T(128)}, u32[]{:S(2)}) copy-start(u32[32]{0:T(128)} %constant.320) | copy-start | bytes 388
  667.8 161.0 %copy-start.5 = (f32[1024,256]{1,0:T(8,128)S(1)}, f32[1024,256]{1,0:T(8,128)}, u32[]{:S(2)}) copy-start(f32[1024,256]{1,0:T(8,128)} %all-reduce.11.cloned.1.call-done) | copy-start | bytes 3145732
  668.9 160.0 %all-gather.10.cloned.1.call-start = ((), (), s32[]{:S(2)}) async-start(), calls=%async_computation.6 | async-start | bytes 1179648 | tf_op jit(solution)/shard_map/all_gather | solution.py:162
  778.7 164.2 %all-reduce.15.cloned.1.call-start = ((), (), s32[]{:S(2)}) async-start(), calls=%async_computation.7 | async-start | bytes 2097152 | tf_op jit(solution)/shard_map/psum | solution.py:14
  835.6 24.3 %slice-start = ((f32[1024,256]{1,0:T(8,128)}), f32[768,256]{1,0:T(8,128)S(1)}, s32[]{:S(2)}) async-start(f32[1024,256]{1,0:T(8,128)} %all-reduce.11.cloned.1.call-done), calls=%async_computation.10 | async-start | bytes 1572864 | tf_op jit(solution)/shard_map/slice | solution.py:182
  835.6 107.3 %copy-start.8 = (f32[128,256]{1,0:T(8,128)S(1)}, f32[128,256]{1,0:T(8,128)}, u32[]{:S(2)}) copy-start(f32[128,256]{1,0:T(8,128)} %convolution_subtract_fusion.9) | copy-start | bytes 393220
  835.6 109.5 %copy-start.6 = (f32[1024,256]{1,0:T(8,128)S(1)}, f32[1024,256]{1,0:T(8,128)}, u32[]{:S(2)}) copy-start(f32[1024,256]{1,0:T(8,128)} %all-reduce.13.cloned.1.call-done) | copy-start | bytes 3145732
  835.6 135.3 %all-gather.12.cloned.1.call-start = ((), (), s32[]{:S(2)}) async-start(), calls=%async_computation.8 | async-start | bytes 1179648 | tf_op jit(solution)/shard_map/all_gather | solution.py:162
  945.0 118.2 %all-reduce.17.cloned.1.call-start = ((), (), s32[]{:S(2)}) async-start(), calls=%async_computation.9 | async-start | bytes 2097152 | tf_op jit(solution)/shard_map/psum | solution.py:14
  (210 other events, 403.8 us)
Sparse Core Ops, SparseCore 0:
  471.3 24.5 reduce-scatter.1
  498.1 20.4 all-gather.5
  584.7 50.3 all-reduce.10
  637.3 22.2 all-gather.7
  669.1 107.4 all-reduce.12
  778.8 22.0 all-gather.9
  835.7 107.1 all-reduce.14
  945.1 22.4 all-gather.11
  976.9 86.2 all-reduce.16
where the time goes:
time: 1110 us; the launch traced here: 1100 us
  waiting for transfers between devices  370 us (33%)
  local copies, waits for them, and re-layouts  355 us (32%)
  other arithmetic  216 us (19%)
  matrix products  66.7 us (6%)
  blocking collectives  48.6 us (4%)
  loops' own time  27.1 us (2%)
  between operations  14.5 us (1%)
    psum x4, waiting for transfers between devices, from_root(): return lax.psum(kept, axis)  302 us
    another operation x13, other arithmetic, on_device(): lax.linalg.triangular_solve(factored[first_row:end_row], gradient[first_r...  80.8 us
    mul x96, local copies, waits for them, and re-layouts, block_terms(): schur = schur + selector[view][:, None, None, :] * products[view][None]  77.7 us
    mul x80, local copies, waits for them, and re-layouts, block_terms(): schur = selector[0][:, None, None, :] * products[0][None]  61.6 us
    all_gather x4, waiting for transfers between devices, on_device(): column = lax.all_gather(held, ('region', 'row'), axis=0, tiled=True)  43.4 us
    all_gather x1, blocking collectives, on_device(): gathered = lax.all_gather(grad_piece, ('region', 'col'), axis=0, tiled=True)  37 us
    dynamic_slice x32, local copies, waits for them, and re-layouts, block_step(): cam = lax.dynamic_slice_in_dim(cam_jac, start, BLOCK, 3)  35.4 us
    another operation x6, other arithmetic, panel_factor(): chol_block = jnp.linalg.cholesky(column[first_row:end_row])  34 us
  transfers between devices with their start and end apart: 9, of which 7 were waited for; matrix products, arithmetic and copies ran while one was open for 7% of the time, Pallas kernels for 0%

commit v1 on v0

--- a/solution.py
+++ b/solution.py
@@ -9,9 +9,15 @@
 point_damping = 0.5
 
 
+def add_all(value, name):
+    parts = lax.all_gather(value, name, axis=0, tiled=False)
+    total = parts.sum(axis=0)
+    return total
+
+
 def from_root(value, axis, source):
     kept = jnp.where(lax.axis_index(axis) == source, value, 0).astype(value.dtype)
-    return lax.psum(kept, axis)
+    return add_all(kept, axis)
 
 
 def lower_solve(factor_parts, first, second, third):

time: 1110 us -> 1180 us (1.063)
  blocking collectives: 48.6 us -> 85.5 us
  other arithmetic: 216 us -> 228 us
    psum x4 -> x0, waiting for transfers between devices: 302 us -> none  [from_root(): return lax.psum(kept, axis)]
    all_gather x0 -> x4, waiting for transfers between devices: none -> 267 us  [add_all(): parts = lax.all_gather(value, name, axis=0, tiled=False)]
    all_gather x4, waiting for transfers between devices: 43.4 us -> 87.9 us  [on_device(): column = lax.all_gather(held, ('region', 'row'), axis=0, tiled=True)]
    all_gather x1, blocking collectives: 37 us -> 75 us  [on_device(): gathered = lax.all_gather(grad_piece, ('region', 'col'), axis=0, tiled=True)]
  transfers between devices with their start and end apart: 9 -> 9, of which waited for: 7 -> 8; matrix products, arithmetic and copies ran while one was open for 7% -> 8% of each run, Pallas kernels for 0% -> 0%
where the time goes in v1:
time: 1180 us; the launch traced here: 1160 us
  waiting for transfers between devices  380 us (32%)
  local copies, waits for them, and re-layouts  357 us (30%)
  other arithmetic  228 us (19%)
  blocking collectives  85.5 us (7%)
  matrix products  71.8 us (6%)
  loops' own time  25.9 us (2%)
  between operations  14.5 us (1%)
    all_gather x4, waiting for transfers between devices, add_all(): parts = lax.all_gather(value, name, axis=0, tiled=False)  267 us
    all_gather x4, waiting for transfers between devices, on_device(): column = lax.all_gather(held, ('region', 'row'), axis=0, tiled=True)  87.9 us
    another operation x13, other arithmetic, on_device(): lax.linalg.triangular_solve(factored[first_row:end_row], gradient[first_r...  82.3 us
    mul x96, local copies, waits for them, and re-layouts, block_terms(): schur = schur + selector[view][:, None, None, :] * products[view][None]  77.7 us
    all_gather x1, blocking collectives, on_device(): gathered = lax.all_gather(grad_piece, ('region', 'col'), axis=0, tiled=True)  75 us
    mul x80, local copies, waits for them, and re-layouts, block_terms(): schur = selector[0][:, None, None, :] * products[0][None]  61.6 us
    dynamic_slice x32, local copies, waits for them, and re-layouts, block_step(): cam = lax.dynamic_slice_in_dim(cam_jac, start, BLOCK, 3)  35.4 us
    another operation x6, other arithmetic, panel_factor(): chol_block = jnp.linalg.cholesky(column[first_row:end_row])  34 us
  transfers between devices with their start and end apart: 9, of which 8 were waited for; matrix products, arithmetic and copies ran while one was open for 8% of the time, Pallas kernels for 0%

profile of v1, /device:TPU:0, one launch (start us, length us, event | category | flops | bytes accessed | tf_op | source)
XLA Modules:
  0.0 1164.0 jit_solution(16715543250556052876)
XLA Ops:
  11.4 459.1 %while.32 = (s32[]{:T(128)}, f32[512,256]{1,0:T(8,128)}, f32[256]{0:T(256)}, f32[3,4096]{1,0:T(4,128)S(1)}, f32[4096]{0:T(1024)}, /*index=5*/bf16[3,2,256,4096]{...) while((s32[]{:T(128)}, f32[512,256]{1,0:T(8,128)}, ...), condition=%wide.region_10.11_spmd.clone, body=%wide.region_0.10_spmd.clone.sunk | while | flops 252784384 | bytes 64036492 | solution.py:146
  470.6 24.7 %reduce-scatter.2.cloned.1.call-done = f32[128,256]{1,0:T(8,128)} async-done(((f32[512,256]{1,0:T(8,128)}), f32[128,256]{1,0:T(8,128)}) %reduce-scatter.2.cloned.1.call-update) | async-done | bytes 131088 | tf_op jit(solution)/shard_map/reduce_scatter | solution.py:148
  497.0 21.0 %all-gather.14.cloned.1.call-done = f32[1024,256]{1,0:T(8,128)} async-done(((f32[128,256]{1,0:T(8,128)}), f32[1024,256]{1,0:T(8,128)}) %all-gather.14.cloned.1.call-update) | async-done | bytes 1048592 | tf_op jit(solution)/shard_map/all_gather | solution.py:168
  518.0 64.8 %conditional.4 = (f32[1024,256]{1,0:T(8,128)S(1)}) conditional(s32[]{:T(128)} %convert_element_type.162, () %tuple.57, f32[1024,256]{1,0:T(8,128)} %all-gather.14.cloned.1.call-done), branch_computations={%region_12.13_spmd, %region_13.0_spmd} | conditional | flops 504480000 | bytes 15862003 | solution.py:169
  520.7 11.7 %cholesky.214 = f32[128,128]{1,0:T(8,128)S(1)} custom-call(f32[128,128]{1,0:T(8,128)S(1)} %cholesky.346), custom_call_target="Cholesky" | custom-call | tf_op jit(solution)/shard_map/cond/branch_1_fun/jit(cholesky)/cholesky | solution.py:82
  532.5 9.8 custom-call.27
  542.8 11.7 %cholesky.231 = f32[128,128]{1,0:T(8,128)S(1)} custom-call(f32[128,128]{1,0:T(8,128)S(1)} %convolution_subtract_fusion.1), custom_call_target="Cholesky" | custom-call | tf_op jit(solution)/shard_map/cond/branch_1_fun/jit(cholesky)/cholesky | solution.py:82
  556.6 3.9 while.29
  560.6 19.7 %custom-call.16 = f32[2,128,128]{1,2,0:T(8,128)S(1)} custom-call(f32[2,128,128]{2,1,0:T(8,128)S(1)} %get-tuple-element.256), custom_call_target="InvertDiagBlocksLowerTriangular" | custom-call | tf_op jit(solution)/shard_map/cond/branch_1_fun/triangular_solve | solution.py:86
  583.9 50.5 %all-gather.22.cloned.1.call-done = f32[4096,256]{1,0:T(8,128)} async-done(((f32[1024,256]{1,0:T(8,128)}), f32[4096,256]{1,0:T(8,128)}) %all-gather.22.cloned.1.call-update) | async-done | bytes 4194320 | tf_op jit(solution)/shard_map/all_gather | solution.py:13
  634.5 2.6 reduce_sum.177
  638.2 22.3 %all-gather.16.cloned.1.call-done = f32[1024,256]{1,0:T(8,128)} async-done(((f32[128,256]{1,0:T(8,128)}), f32[1024,256]{1,0:T(8,128)}) %all-gather.16.cloned.1.call-update) | async-done | bytes 1048592 | tf_op jit(solution)/shard_map/all_gather | solution.py:168
  660.5 8.3 conditional.5
  670.0 107.3 %all-gather.24.cloned.1.call-done = f32[4096,256]{1,0:T(8,128)} async-done(((f32[1024,256]{1,0:T(8,128)}), f32[4096,256]{1,0:T(8,128)}) %all-gather.24.cloned.1.call-update) | async-done | bytes 4194320 | tf_op jit(solution)/shard_map/all_gather | solution.py:13
  777.2 2.6 reduce_sum.178
  781.0 22.3 %all-gather.18.cloned.1.call-done = f32[1024,256]{1,0:T(8,128)} async-done(((f32[128,256]{1,0:T(8,128)}), f32[1024,256]{1,0:T(8,128)}) %all-gather.18.cloned.1.call-update) | async-done | bytes 1048592 | tf_op jit(solution)/shard_map/all_gather | solution.py:168
  803.3 8.8 conditional.6
  813.3 109.6 %all-gather.26.cloned.1.call-done = f32[4096,256]{1,0:T(8,128)} async-done(((f32[1024,256]{1,0:T(8,128)}), f32[4096,256]{1,0:T(8,128)}) %all-gather.26.cloned.1.call-update) | async-done | bytes 4194320 | tf_op jit(solution)/shard_map/all_gather | solution.py:13
  922.9 2.6 reduce_sum.179
  926.7 22.3 %all-gather.20.cloned.1.call-done = f32[1024,256]{1,0:T(8,128)} async-done(((f32[128,256]{1,0:T(8,128)}), f32[1024,256]{1,0:T(8,128)}) %all-gather.20.cloned.1.call-update) | async-done | bytes 1048592 | tf_op jit(solution)/shard_map/all_gather | solution.py:168
  950.9 10.4 all-reduce.5
  962.0 75.0 %all-gather.4 = f32[16,1,64]{2,1,0:T(1,128)S(1)} all-gather(f32[1,1,64]{2,1,0:T(1,128)S(1)} %dynamic-slice_bitcast_fusion.1), channel_id=1, replica_groups=mesh['region'=4,'row'=2,'col'=4] {'region','col'}, dimensions={0}, use_global_device_ids=true | all-gather | bytes 4352 | tf_op jit(solution)/shard_map/all_gather | solution.py:153
  1038.2 4.3 while.33
  1042.6 20.3 %custom-call.31 = f32[2,128,128]{1,2,0:T(8,128)} custom-call(f32[2,128,128]{2,1,0:T(8,128)S(1)} %get-tuple-element.332), custom_call_target="InvertDiagBlocksLowerTriangular" | custom-call | tf_op jit(solution)/shard_map/triangular_solve/custom-call.6 | solution.py:180
  1065.1 1.9 fusion.72
  1067.9 4.0 while.34
  1071.9 20.3 %custom-call.32 = f32[2,128,128]{1,2,0:T(8,128)} custom-call(f32[2,128,128]{2,1,0:T(8,128)S(1)} %get-tuple-element.333), custom_call_target="InvertDiagBlocksLowerTriangular" | custom-call | tf_op jit(solution)/shard_map/triangular_solve/custom-call.6 | solution.py:180
  1096.9 5.3 while.35
  1102.2 20.3 %custom-call.33 = f32[2,128,128]{1,2,0:T(8,128)} custom-call(f32[2,128,128]{2,1,0:T(8,128)S(1)} %get-tuple-element.334), custom_call_target="InvertDiagBlocksLowerTriangular" | custom-call | tf_op jit(solution)/shard_map/triangular_solve/custom-call.6 | solution.py:180
  1126.1 3.6 reduce_sum.180
  1132.3 4.1 while.36
  1136.4 19.7 %custom-call.34 = f32[2,128,128]{1,2,0:T(8,128)S(1)} custom-call(f32[2,128,128]{2,1,0:T(8,128)S(1)} %get-tuple-element.335), custom_call_target="InvertDiagBlocksLowerTriangular" | custom-call | tf_op jit(solution)/shard_map/triangular_solve/custom-call.6 | solution.py:180
  (1513 shorter events, 511.5 us)
Async XLA Ops:
  7.2 488.1 %reduce-scatter.2.cloned.1.call-start = ((), (), s32[]{:S(2)}) async-start(), calls=%async_computation.1 | async-start | bytes 655360 | tf_op jit(solution)/shard_map/reduce_scatter | solution.py:148
  11.4 5.8 copy-start.17
  32.4 3.5 copy-start
  32.4 3.5 copy-start.1
  40.1 5.8 copy-start.17
  68.8 5.8 copy-start.17
  97.5 5.8 copy-start.17
  126.2 5.8 copy-start.17
  154.9 5.8 copy-start.17
  183.6 5.8 copy-start.17
  212.3 5.8 copy-start.17
  241.0 5.8 copy-start.17
  269.7 5.8 copy-start.17
  298.4 5.8 copy-start.17
  327.1 5.8 copy-start.17
  355.8 5.8 copy-start.17
  384.5 5.8 copy-start.17
  413.1 5.8 copy-start.17
  441.8 5.8 copy-start.17
  470.6 47.4 %all-gather.14.cloned.1.call-start = ((), (), s32[]{:S(2)}) async-start(), calls=%async_computation.2 | async-start | bytes 1179648 | tf_op jit(solution)/shard_map/all_gather | solution.py:168
  497.0 137.5 %all-gather.22.cloned.1.call-start = ((), (), s32[]{:S(2)}) async-start(), calls=%async_computation.6 | async-start | bytes 5242880 | tf_op jit(solution)/shard_map/all_gather | solution.py:13
  519.5 60.8 %copy-start.7 = (f32[1024,256]{1,0:T(8,128)S(1)}, f32[1024,256]{1,0:T(8,128)}, u32[]{:S(2)}) copy-start(f32[1024,256]{1,0:T(8,128)} %param.4) | copy-start | bytes 3145732 | tf_op jit(solution)/shard_map/cond
  583.9 76.7 %all-gather.16.cloned.1.call-start = ((), (), s32[]{:S(2)}) async-start(), calls=%async_computation.3 | async-start | bytes 1179648 | tf_op jit(solution)/shard_map/all_gather | solution.py:168
  638.1 139.1 %all-gather.24.cloned.1.call-start = ((), (), s32[]{:S(2)}) async-start(), calls=%async_computation.7 | async-start | bytes 5242880 | tf_op jit(solution)/shard_map/all_gather | solution.py:13
  669.9 133.4 %all-gather.18.cloned.1.call-start = ((), (), s32[]{:S(2)}) async-start(), calls=%async_computation.4 | async-start | bytes 1179648 | tf_op jit(solution)/shard_map/all_gather | solution.py:168
  780.9 142.0 %all-gather.26.cloned.1.call-start = ((), (), s32[]{:S(2)}) async-start(), calls=%async_computation.8 | async-start | bytes 5242880 | tf_op jit(solution)/shard_map/all_gather | solution.py:13
  813.2 135.8 %all-gather.20.cloned.1.call-start = ((), (), s32[]{:S(2)}) async-start(), calls=%async_computation.5 | async-start | bytes 1179648 | tf_op jit(solution)/shard_map/all_gather | solution.py:168
  925.5 23.5 %copy-start.5 = (f32[1024,256]{1,0:T(8,128)}, f32[1024,256]{1,0:T(8,128)S(1)}, u32[]{:S(2)}) copy-start(f32[1024,256]{1,0:T(8,128)S(1)} %reduce_sum.179) | copy-start | bytes 3145732
  926.6 199.5 %all-gather.28.cloned.1.call-start = ((), (), s32[]{:S(2)}) async-start(), calls=%async_computation.9 | async-start | bytes 5242880 | tf_op jit(solution)/shard_map/all_gather | solution.py:13
  1042.6 53.6 %copy-start.6 = (f32[1024,256]{1,0:T(8,128)S(1)}, f32[1024,256]{1,0:T(8,128)}, u32[]{:S(2)}) copy-start(f32[1024,256]{1,0:T(8,128)} %copy-done.5) | copy-start | bytes 3145732
  1071.9 24.2 %copy-start.22 = (s32[2,2]{1,0:T(2,128)}, s32[2,2]{1,0:T(2,128)S(1)}, u32[]{:S(2)}) copy-start(s32[2,2]{1,0:T(2,128)S(1)} %get-tuple-element.1074) | copy-start | bytes 52
  1126.1 6.2 copy-start.23
  (211 other events, 394.2 us)
Sparse Core Ops, SparseCore 0:
  470.7 24.5 reduce-scatter.1
  497.5 20.4 all-gather.13
  584.0 50.4 all-gather.21
  638.3 22.2 all-gather.15
  670.0 107.1 all-gather.23
  781.1 22.2 all-gather.17
  813.3 109.5 all-gather.25
  926.8 22.2 all-gather.19
  950.9 89.4 all-gather.27
